TPU v7x, 128 devices: a whole 4x4x4 slice. The times are simulated.
128 devices in a mesh: ctx: 8 (over z, core), tp: 16 (over x, y).
Axes of the slice: x: 4, y: 4, z: 4, core: 2. Of those that a mesh axis runs over, the one named last changes fastest.
Arguments:
- inputs: bfloat16 [2048, 8192], P(('ctx', 'tp')), may hold values from -6 to 6
- query_weight: bfloat16 [8192, 8192], P(None, 'tp'), may hold values from -0.0625 to 0.0625
- key_weight: bfloat16 [8192, 8192], P(None, 'tp'), may hold values from -0.0625 to 0.0625
- value_weight: bfloat16 [8192, 8192], P(None, 'tp'), may hold values from -0.0625 to 0.0625
- filter_taps: float32 [128, 8192], P(None, 'tp'), may hold values from -0.45 to 0.45
- out_grad: bfloat16 [2048, 8192], P('ctx', 'tp'), may hold values from -1.5 to 1.5
Outputs:
- mixed: bfloat16 [2048, 8192], P('ctx', 'tp')
- inputs_grad: bfloat16 [2048, 8192], P(('ctx', 'tp'))
- filter_grad: float32 [128, 8192], P(None, 'tp')
All inputs are finite; a program needn't handle non-finite values.
Results may differ from a plain program's by a relative error of at most 0.025.
Values may be sent and summed in bfloat16 or wider, within the bound.
A program may use at most 128 MiB of HBM per device.

v0:
```python
import jax
import jax.numpy as jnp
from jax import lax
from jax.sharding import PartitionSpec as P


def from_behind(block, axis, distance):
    devices = range(lax.axis_size(axis))
    route = [(i - distance, i) for i in devices if i - distance in devices]
    return lax.ppermute(block, axis, route)


def forward_filter(padded, filter_taps, length):
    taps = filter_taps.shape[0]
    total = jnp.zeros((length, padded.shape[1]), jnp.float32)
    for offset in range(taps):
        start = taps - 1 - offset
        total = total + filter_taps[offset] * padded[start : start + length]
    return total


def backward_filter(padded, filter_taps, length):
    taps = filter_taps.shape[0]
    total = jnp.zeros((length, padded.shape[1]), jnp.float32)
    for offset in range(taps):
        total = total + filter_taps[offset] * padded[offset : offset + length]
    return total


def tap_products(grad_rows, padded, taps, length):
    rows_out = []
    for offset in range(taps):
        start = taps - 1 - offset
        rows_out.append(jnp.sum(grad_rows * padded[start : start + length], axis=0))
    return jnp.stack(rows_out)


def contract(left, right):
    return lax.dot_general(
        left, right, (((1,), (1,)), ((), ())), preferred_element_type=jnp.float32
    )


def on_device(inputs, query_weight, key_weight, value_weight, filter_taps, out_grad):
    group = query_weight.shape[1]
    taps = filter_taps.shape[0]
    margin = taps - 1
    own_rows = inputs.shape[0]
    piece = lax.all_gather(inputs, "tp", axis=0, tiled=True)
    query_part = jnp.dot(piece, query_weight, preferred_element_type=jnp.float32)
    keys_part = jnp.dot(piece, key_weight, preferred_element_type=jnp.float32)
    values_part = jnp.dot(piece, value_weight, preferred_element_type=jnp.float32)
    projected = jnp.concatenate([query_part, keys_part, values_part], axis=1).astype(jnp.bfloat16)
    length = projected.shape[0]
    query = projected[:, :group]
    keys = projected[:, group : 2 * group]
    values = projected[:, 2 * group :]
    product = (keys.astype(jnp.float32) * values.astype(jnp.float32)).astype(jnp.bfloat16)
    grad_f32 = out_grad.astype(jnp.float32)
    conv_in_grad = (grad_f32 * query.astype(jnp.float32)).astype(jnp.bfloat16)
    tail_part = from_behind(product[length - margin :], "ctx", 1)
    head_part = from_behind(conv_in_grad[:margin], "ctx", -1)
    padded_prod = jnp.concatenate([tail_part, product], axis=0).astype(jnp.float32)
    conv = forward_filter(padded_prod, filter_taps, length)
    mixed = (query.astype(jnp.float32) * conv).astype(jnp.bfloat16)
    query_grad = (grad_f32 * conv).astype(jnp.bfloat16)
    padded_grad = jnp.concatenate([conv_in_grad, head_part], axis=0).astype(jnp.float32)
    product_grad = backward_filter(padded_grad, filter_taps, length)
    keys_grad = (product_grad * values.astype(jnp.float32)).astype(jnp.bfloat16)
    values_grad = (product_grad * keys.astype(jnp.float32)).astype(jnp.bfloat16)
    local_taps = tap_products(conv_in_grad.astype(jnp.float32), padded_prod, taps, length)
    filter_grad = lax.psum(local_taps.astype(jnp.bfloat16), "ctx").astype(jnp.float32)
    query_rows = lax.slice_in_dim(query_grad, 0, lax.axis_size("tp") * own_rows, axis=0)
    keys_rows = lax.slice_in_dim(keys_grad, 0, lax.axis_size("tp") * own_rows, axis=0)
    values_rows = lax.slice_in_dim(values_grad, 0, lax.axis_size("tp") * own_rows, axis=0)
    total = contract(query_rows, query_weight)
    total = total + contract(keys_rows, key_weight)
    summed = lax.psum_scatter(
        (total + contract(values_rows, value_weight)).astype(jnp.bfloat16),
        "tp",
        scatter_dimension=0,
        tiled=True,
    )
    return (mixed, summed, filter_grad)


def solution(mesh):
    in_specs = (
        P(("ctx", "tp"), None),
        P(None, "tp"),
        P(None, "tp"),
        P(None, "tp"),
        P(None, "tp"),
        P("ctx", "tp"),
    )
    out_specs = (P("ctx", "tp"), P(("ctx", "tp"), None), P(None, "tp"))
    return jax.shard_map(
        on_device, mesh=mesh, in_specs=in_specs, out_specs=out_specs, check_vma=False
    )
```

profile of v0, /device:TPU:0, one launch (start us, length us, event | category | flops | bytes accessed | tf_op | source)
XLA Modules:
  0.0 267.7 jit_solution(11515920868183889877)
XLA Ops:
  7.2 0.7 all-gather.2.cloned.1.call-update
  7.9 1.2 fusion.268
  9.2 1.3 fusion.267
  10.4 1.2 fusion.266
  11.7 1.2 fusion.265
  12.9 1.1 fusion.264
  14.0 1.7 fusion.269
  15.7 48.3 %all-gather.2.cloned.1.call-done = bf16[256,8192]{1,0:T(8,128)(2,1)} async-done(((bf16[16,8192]{1,0:T(8,128)(2,1)}), bf16[256,8192]{1,0:T(8,128)(2,1)}) %all-gather.2.cloned.1.call-update) | async-done | bytes 4194320 | tf_op jit(solution)/shard_map/all_gather | solution.py:49
  64.0 7.1 %fusion.1 = f32[256,512]{1,0:T(8,128)S(1)} fusion(bf16[256,8192]{1,0:T(8,128)(2,1)} %all-gather.2.cloned.1.call-done, bf16[8192,512]{1,0:T(8,128)(2,1)} %param.9), kind=kOutput, calls=%fused_computation.132 | convolution fusion | flops 2147745792 | bytes 13107200 | tf_op jit(solution)/shard_map/dot_general | solution.py:52
  71.2 6.8 %multiply_convert_fusion.3 = (bf16[256,512]{1,0:T(8,128)(2,1)S(1)}, f32[256,512]{1,0:T(8,128)}) fusion(f32[256,512]{1,0:T(8,128)S(1)} %fusion.1, bf16[256,8192]{1,0:T(8,128)(2,1)S(1)} %copy-done.20, bf16[8192,512]{1,0:T(8,128)(2,1)} %param.8), kind=kOutput, calls=%fused_computation.528 | convolution fusion | flops 2148007936 | bytes 13893632 | tf_op jit(solution)/shard_map/dot_general | solution.py:51
  78.0 1.7 collective-permute-start
  79.8 1.7 fusion.270
  81.5 0.1 maximum_convert_fusion
  81.6 16.5 %multiply_convert_fusion.2 = (bf16[256,512]{1,0:T(8,128)(2,1)}, f32[256,512]{1,0:T(8,128)}, f32[256,512]{1,0:T(8,128)}) fusion(f32[383,512]{1,0:T(8,128)S(1)} %maximum_convert_fusion, f32[512]{0:T(512)} %bitcast.391, f32[512]{0:T(512)} %bitcast.393, f32[512]{0:T(512)S(1)} %bitcast.293, f32[512]{0:T(512)S(1)} %bitcast.295, f32[512]{0:T(512)S(1)} %bitcast.297, ...), kind=kOutput, calls=%fused_computation.526 | convolution fusion | flops 2181431296 | bytes 81264640 | tf_op jit(solution)/shard_map/dot_general | solution.py:50
  98.1 2.1 fusion.127
  100.2 0.2 fusion.126
  100.4 1.0 fusion.128
  101.4 1.0 fusion.129
  102.4 1.0 fusion.130
  103.5 1.1 fusion.131
  104.5 1.1 fusion.132
  105.6 1.0 fusion.133
  108.1 10.1 %stack.644 = bf16[128,512]{1,0:T(8,128)(2,1)} concatenate(bf16[1,512]{1,0:T(2,128)(2,1)S(1)} %stack.516, bf16[1,512]{1,0:T(2,128)(2,1)S(1)} %stack.517, bf16[1,512]{1,0:T(2,128)(2,1)S(1)} %stack.518, bf16[1,512]{1,0:T(2,128)(2,1)S(1)} %stack.519, bf16[1,512]{1,0:T(2,128)(2,1)S(1)} %stack.520, bf16[1,512]{1,0:T(2,128)(2,1)S(1)} %stack.521, bf16[1,512]{1,0:T(2,128)(2,1)S(1)} %stack.522, ...), dimensions={0} | concatenate | bytes 262144 | tf_op jit(solution)/shard_map/stack | solution.py:35
  118.3 1.3 collective-permute-start.1
  119.8 5.8 %fusion.261 = f32[256,8192]{1,0:T(8,128)S(1)} fusion(bf16[8192,512]{1,0:T(8,128)(2,1)} %param.7, f32[256,512]{1,0:T(8,128)S(1)} %copy-done.4, bf16[256,512]{1,0:T(8,128)(2,1)S(1)} %copy-done), kind=kOutput, calls=%fused_computation.532 | convolution fusion | flops 2147876864 | bytes 17563648 | tf_op jit(solution)/shard_map/dot_general | solution.py:39
  125.6 0.1 maximum_convert_fusion.1
  125.8 12.3 %fusion.134 = f32[256,512]{1,0:T(8,128)S(1)} fusion(f32[383,512]{1,0:T(8,128)S(1)} %maximum_convert_fusion.1, f32[512]{0:T(512)S(1)} %bitcast.392, f32[512]{0:T(512)S(1)} %bitcast.394, f32[512]{0:T(512)S(1)} %bitcast.294, f32[512]{0:T(512)S(1)} %bitcast.296, f32[512]{0:T(512)S(1)} %bitcast.298, f32[512]{0:T(512)S(1)} %bitcast.300, f32[512]{0:T(512)S(1)} %bitcast.302, ...), kind=kLoop, calls=%fused_computation.270 | loop fusion | flops 33423360 | bytes 67895296 | tf_op jit(solution)/shard_map/add | solution.py:26
  138.2 9.1 %convolution_add_fusion.1 = f32[256,8192]{1,0:T(8,128)} fusion(f32[256,8192]{1,0:T(8,128)S(1)} %fusion.261, bf16[8192,512]{1,0:T(8,128)(2,1)} %param.8, f32[256,512]{1,0:T(8,128)S(1)} %fusion.134, f32[256,512]{1,0:T(8,128)S(1)} %copy-done.3), kind=kOutput, calls=%fused_computation.129 | convolution fusion | flops 2149842944 | bytes 26214400 | tf_op jit(solution)/shard_map/dot_general | solution.py:39
  147.3 10.2 %fusion = bf16[256,8192]{1,0:T(8,128)(2,1)} fusion(f32[256,8192]{1,0:T(8,128)} %convolution_add_fusion.1, bf16[8192,512]{1,0:T(8,128)(2,1)} %param.9, f32[256,512]{1,0:T(8,128)S(1)} %fusion.134, f32[256,512]{1,0:T(8,128)S(1)} %copy-done.1), kind=kOutput, calls=%fused_computation.130 | convolution fusion | flops 2151940096 | bytes 22020096 | tf_op jit(solution)/shard_map/dot_general | solution.py:39
  157.5 23.0 %all-reduce.2.cloned.1.call-done = bf16[128,512]{1,0:T(8,128)(2,1)} async-done(((bf16[128,512]{1,0:T(8,128)(2,1)}), bf16[128,512]{1,0:T(8,128)(2,1)}) %all-reduce.2.cloned.1.call-update) | async-done | bytes 131088 | tf_op jit(solution)/shard_map/psum | solution.py:72
  180.4 1.6 convert_element_type.64
  182.1 79.1 %reduce-scatter.2.cloned.1.call-done = bf16[16,8192]{1,0:T(8,128)(2,1)} async-done(((bf16[256,8192]{1,0:T(8,128)(2,1)}), bf16[16,8192]{1,0:T(8,128)(2,1)}) %reduce-scatter.2.cloned.1.call-update) | async-done | bytes 262160 | tf_op jit(solution)/shard_map/reduce_scatter | solution.py:78
  (184 shorter events, 0.9 us)
Async XLA Ops:
  7.2 56.9 %all-gather.2.cloned.1.call-start = ((), (), s32[]{:S(2)}) async-start(), calls=%async_computation.1 | async-start | bytes 4456448 | tf_op jit(solution)/shard_map/all_gather | solution.py:49
  7.9 172.5 %all-reduce.2.cloned.1.call-start = ((), (), s32[]{:S(2)}) async-start(), calls=%async_computation.3 | async-start | bytes 262144 | tf_op jit(solution)/shard_map/psum | solution.py:72
  64.0 7.1 %copy-start.20 = (bf16[256,8192]{1,0:T(8,128)(2,1)S(1)}, bf16[256,8192]{1,0:T(8,128)(2,1)}, u32[]{:S(2)}) copy-start(bf16[256,8192]{1,0:T(8,128)(2,1)} %all-gather.2.cloned.1.call-done) | copy-start | bytes 12582916
  64.0 17.5 %slice-start = ((s8[8388608]{0:T(1024)(128)(4,1)}), s8[4194304]{0:T(1024)(128)(4,1)S(1)}, s32[]{:S(2)}) async-start(s8[8388608]{0:T(1024)(128)(4,1)} %bitcast.137), calls=%async_computation.4 | async-start | bytes 8388608
  71.2 6.8 %copy-start.2 = (f32[256,512]{1,0:T(8,128)}, f32[256,512]{1,0:T(8,128)S(1)}, u32[]{:S(2)}) copy-start(f32[256,512]{1,0:T(8,128)S(1)} %fusion.1) | copy-start | bytes 1572868
  71.2 10.4 %slice-start.1 = ((s8[8388608]{0:T(1024)(128)(4,1)}), s8[4194304]{0:T(1024)(128)(4,1)S(1)}, s32[]{:S(2)}) async-start(s8[8388608]{0:T(1024)(128)(4,1)} %bitcast.137), calls=%async_computation.5 | async-start | bytes 8388608
  78.0 3.4 %collective-permute-start = (bf16[127,512]{1,0:T(8,128)(2,1)S(1)}, bf16[127,512]{1,0:T(8,128)(2,1)S(1)}, u32[]{:S(2)}, u32[]{:S(2)}) collective-permute-start(bf16[127,512]{1,0:T(8,128)(2,1)S(1)} %slice.1812), channel_id=1, source_target_pairs={{0,16},{16,32},{32,48},{48,64},{64,80},{80,96},{96,112},{1,17},{17... | collective-permute-start | bytes 390152 | tf_op jit(solution)/shard_map/ppermute | solution.py:10
  81.6 16.5 %copy-start = (bf16[256,512]{1,0:T(8,128)(2,1)S(1)}, bf16[256,512]{1,0:T(8,128)(2,1)}, u32[]{:S(2)}) copy-start(bf16[256,512]{1,0:T(8,128)(2,1)} %param.11) | copy-start | bytes 786436
  104.5 15.1 %copy-start.4 = (f32[256,512]{1,0:T(8,128)S(1)}, f32[256,512]{1,0:T(8,128)}, u32[]{:S(2)}) copy-start(f32[256,512]{1,0:T(8,128)} %get-tuple-element.133) | copy-start | bytes 1572868
  118.3 142.9 %reduce-scatter.2.cloned.1.call-start = ((), (), s32[]{:S(2)}) async-start(), calls=%async_computation.2 | async-start | bytes 4456448 | tf_op jit(solution)/shard_map/reduce_scatter | solution.py:78
  118.3 7.2 %collective-permute-start.1 = (bf16[127,512]{1,0:T(8,128)(2,1)S(1)}, bf16[127,512]{1,0:T(8,128)(2,1)S(1)}, u32[]{:S(2)}, u32[]{:S(2)}) collective-permute-start(bf16[127,512]{1,0:T(8,128)(2,1)S(1)} %slice.1941), channel_id=1, source_target_pairs={{16,0},{32,16},{48,32},{64,48},{80,64},{96,80},{112,96},{17,1},{33... | collective-permute-start | bytes 390152 | tf_op jit(solution)/shard_map/ppermute | solution.py:10
  119.7 6.0 %copy-start.5 = (f32[1,512]{1,0:T(1,128)S(1)}, f32[1,512]{1,0:T(1,128)}, u32[]{:S(2)}) copy-start(f32[1,512]{1,0:T(1,128)} %get-tuple-element.247) | copy-start | bytes 6148
  119.7 6.0 %copy-start.6 = (f32[1,512]{1,0:T(1,128)S(1)}, f32[1,512]{1,0:T(1,128)}, u32[]{:S(2)}) copy-start(f32[1,512]{1,0:T(1,128)} %get-tuple-element.248) | copy-start | bytes 6148
  119.7 6.0 %copy-start.7 = (f32[1,512]{1,0:T(1,128)S(1)}, f32[1,512]{1,0:T(1,128)}, u32[]{:S(2)}) copy-start(f32[1,512]{1,0:T(1,128)} %get-tuple-element.249) | copy-start | bytes 6148
  119.7 6.0 %copy-start.8 = (f32[1,512]{1,0:T(1,128)S(1)}, f32[1,512]{1,0:T(1,128)}, u32[]{:S(2)}) copy-start(f32[1,512]{1,0:T(1,128)} %get-tuple-element.250) | copy-start | bytes 6148
  119.7 6.0 %copy-start.9 = (f32[1,512]{1,0:T(1,128)S(1)}, f32[1,512]{1,0:T(1,128)}, u32[]{:S(2)}) copy-start(f32[1,512]{1,0:T(1,128)} %get-tuple-element.251) | copy-start | bytes 6148
  119.7 6.0 %copy-start.10 = (f32[1,512]{1,0:T(1,128)S(1)}, f32[1,512]{1,0:T(1,128)}, u32[]{:S(2)}) copy-start(f32[1,512]{1,0:T(1,128)} %get-tuple-element.252) | copy-start | bytes 6148
  119.7 6.0 %copy-start.11 = (f32[1,512]{1,0:T(1,128)S(1)}, f32[1,512]{1,0:T(1,128)}, u32[]{:S(2)}) copy-start(f32[1,512]{1,0:T(1,128)} %get-tuple-element.253) | copy-start | bytes 6148
  119.7 6.0 %copy-start.12 = (f32[1,512]{1,0:T(1,128)S(1)}, f32[1,512]{1,0:T(1,128)}, u32[]{:S(2)}) copy-start(f32[1,512]{1,0:T(1,128)} %get-tuple-element.254) | copy-start | bytes 6148
  119.7 6.0 %copy-start.13 = (f32[1,512]{1,0:T(1,128)S(1)}, f32[1,512]{1,0:T(1,128)}, u32[]{:S(2)}) copy-start(f32[1,512]{1,0:T(1,128)} %get-tuple-element.255) | copy-start | bytes 6148
  119.7 6.0 %copy-start.14 = (f32[1,512]{1,0:T(1,128)S(1)}, f32[1,512]{1,0:T(1,128)}, u32[]{:S(2)}) copy-start(f32[1,512]{1,0:T(1,128)} %get-tuple-element.256) | copy-start | bytes 6148
  119.8 6.0 %copy-start.15 = (f32[1,512]{1,0:T(1,128)S(1)}, f32[1,512]{1,0:T(1,128)}, u32[]{:S(2)}) copy-start(f32[1,512]{1,0:T(1,128)} %get-tuple-element.257) | copy-start | bytes 6148
  119.8 6.0 %copy-start.16 = (f32[1,512]{1,0:T(1,128)S(1)}, f32[1,512]{1,0:T(1,128)}, u32[]{:S(2)}) copy-start(f32[1,512]{1,0:T(1,128)} %get-tuple-element.258) | copy-start | bytes 6148
  119.8 6.0 %copy-start.17 = (f32[1,512]{1,0:T(1,128)S(1)}, f32[1,512]{1,0:T(1,128)}, u32[]{:S(2)}) copy-start(f32[1,512]{1,0:T(1,128)} %get-tuple-element.259) | copy-start | bytes 6148
  119.8 6.0 %copy-start.18 = (f32[1,512]{1,0:T(1,128)S(1)}, f32[1,512]{1,0:T(1,128)}, u32[]{:S(2)}) copy-start(f32[1,512]{1,0:T(1,128)} %get-tuple-element.260) | copy-start | bytes 6148
  119.8 6.0 %copy-start.19 = (f32[1,512]{1,0:T(1,128)S(1)}, f32[1,512]{1,0:T(1,128)}, u32[]{:S(2)}) copy-start(f32[1,512]{1,0:T(1,128)} %get-tuple-element.261) | copy-start | bytes 6148
  125.8 12.4 %copy-start.3 = (f32[256,512]{1,0:T(8,128)S(1)}, f32[256,512]{1,0:T(8,128)}, u32[]{:S(2)}) copy-start(f32[256,512]{1,0:T(8,128)} %copy-done.2) | copy-start | bytes 1572868
  138.2 9.1 %copy-start.1 = (f32[256,512]{1,0:T(8,128)S(1)}, f32[256,512]{1,0:T(8,128)}, u32[]{:S(2)}) copy-start(f32[256,512]{1,0:T(8,128)} %get-tuple-element.263) | copy-start | bytes 1572868
Sparse Core Ops, SparseCore 0:
  10.1 53.8 all-gather.1
  118.4 61.9 all-reduce.1
  184.7 76.3 reduce-scatter.1
where the time goes:
time: 269 us; the launch traced here: 268 us
  waiting for transfers between devices  151 us (56%)
  matrix products  55.4 us (21%)
  other arithmetic  22.6 us (8%)
  local copies, waits for them, and re-layouts  20.4 us (8%)
  between operations  15.1 us (6%)
  starting transfers between devices  3.16 us (1%)
    reduce_scatter x1, waiting for transfers between devices, on_device(): lax.psum_scatter((total + contract(values_rows, value_weight)).astype(jnp...  79.1 us
    all_gather x1, waiting for transfers between devices, on_device(): piece = lax.all_gather(inputs, 'tp', axis=0, tiled=True)  48.3 us
    dot_general x3, matrix products, contract(): lax.dot_general(left, right, (((1,), (1,)), ((), ())), preferred_element_...  25 us
    psum x1, waiting for transfers between devices, on_device(): lax.psum(local_taps.astype(jnp.bfloat16), 'ctx').astype(jnp.float32)  23 us
    dot_general x1, matrix products, on_device(): jnp.dot(piece, query_weight, preferred_element_type=jnp.float32)  16.5 us
    add x1, other arithmetic, backward_filter(): total = total + filter_taps[offset] * padded[offset:offset + length]  12.3 us
    another operation x129, local copies, waits for them, and re-layouts, tap_products(): return jnp.stack(rows_out)  10.8 us
    slice x7, local copies, waits for them, and re-layouts, forward_filter(): total = total + filter_taps[offset] * padded[start:start + length]  9.45 us
  transfers between devices with their start and end apart: 5, of which 3 were waited for; matrix products, arithmetic and copies ran while one was open for 18% of the time, Pallas kernels for 0%

commit v1 on v0

--- a/solution.py
+++ b/solution.py
@@ -69,7 +69,9 @@
     keys_grad = (product_grad * values.astype(jnp.float32)).astype(jnp.bfloat16)
     values_grad = (product_grad * keys.astype(jnp.float32)).astype(jnp.bfloat16)
     local_taps = tap_products(conv_in_grad.astype(jnp.float32), padded_prod, taps, length)
-    filter_grad = lax.psum(local_taps.astype(jnp.bfloat16), "ctx").astype(jnp.float32)
+    filter_grad = jnp.sum(lax.all_gather(local_taps.astype(jnp.bfloat16), "ctx"), axis=0).astype(
+        jnp.float32
+    )
     query_rows = lax.slice_in_dim(query_grad, 0, lax.axis_size("tp") * own_rows, axis=0)
     keys_rows = lax.slice_in_dim(keys_grad, 0, lax.axis_size("tp") * own_rows, axis=0)
     values_rows = lax.slice_in_dim(values_grad, 0, lax.axis_size("tp") * own_rows, axis=0)

time: 269 us -> 246 us (0.914)
  waiting for transfers between devices: 151 us -> 128 us
    psum x1 -> x0, waiting for transfers between devices: 23 us -> none  [on_device(): lax.psum(local_taps.astype(jnp.bfloat16), 'ctx').astype(jnp.float32)]
  transfers between devices with their start and end apart: 5 -> 5, of which waited for: 3 -> 2; matrix products, arithmetic and copies ran while one was open for 18% -> 20% of each run, Pallas kernels for 0% -> 0%
where the time goes in v1:
time: 246 us; the launch traced here: 245 us
  waiting for transfers between devices  128 us (52%)
  matrix products  55.5 us (23%)
  other arithmetic  23.1 us (9%)
  local copies, waits for them, and re-layouts  20.3 us (8%)
  between operations  15.1 us (6%)
  starting transfers between devices  3.16 us (1%)
    reduce_scatter x1, waiting for transfers between devices, on_device(): lax.psum_scatter((total + contract(values_rows, value_weight)).astype(jnp...  78.8 us
    all_gather x1, waiting for transfers between devices, on_device(): piece = lax.all_gather(inputs, 'tp', axis=0, tiled=True)  48.4 us
    dot_general x3, matrix products, contract(): lax.dot_general(left, right, (((1,), (1,)), ((), ())), preferred_element_...  25 us
    dot_general x1, matrix products, on_device(): jnp.dot(piece, query_weight, preferred_element_type=jnp.float32)  16.5 us
    add x1, other arithmetic, backward_filter(): total = total + filter_taps[offset] * padded[offset:offset + length]  12.3 us
    another operation x129, local copies, waits for them, and re-layouts, tap_products(): return jnp.stack(rows_out)  10.8 us
    slice x7, local copies, waits for them, and re-layouts, forward_filter(): total = total + filter_taps[offset] * padded[start:start + length]  9.39 us
    reduce_sum x8, other arithmetic, tap_products(): rows_out.append(jnp.sum(grad_rows * padded[start:start + length], axis=0))  8.45 us
  transfers between devices with their start and end apart: 5, of which 2 were waited for; matrix products, arithmetic and copies ran while one was open for 20% of the time, Pallas kernels for 0%

profile of v1, /device:TPU:0, one launch (start us, length us, event | category | flops | bytes accessed | tf_op | source)
XLA Modules:
  0.0 244.9 jit_solution(1475806103304956271)
XLA Ops:
  7.2 0.7 all-gather.3.cloned.1.call-update
  7.9 1.2 fusion.268
  9.2 1.3 fusion.267
  10.4 1.2 fusion.266
  11.7 1.2 fusion.265
  12.9 1.1 fusion.264
  14.0 1.7 fusion.269
  15.7 48.4 %all-gather.3.cloned.1.call-done = bf16[256,8192]{1,0:T(8,128)(2,1)} async-done(((bf16[16,8192]{1,0:T(8,128)(2,1)}), bf16[256,8192]{1,0:T(8,128)(2,1)}) %all-gather.3.cloned.1.call-update) | async-done | bytes 4194320 | tf_op jit(solution)/shard_map/all_gather | solution.py:49
  64.0 7.1 %fusion.1 = f32[256,512]{1,0:T(8,128)S(1)} fusion(bf16[256,8192]{1,0:T(8,128)(2,1)} %all-gather.3.cloned.1.call-done, bf16[8192,512]{1,0:T(8,128)(2,1)} %param.9), kind=kOutput, calls=%fused_computation.132 | convolution fusion | flops 2147745792 | bytes 13107200 | tf_op jit(solution)/shard_map/dot_general | solution.py:52
  71.2 6.8 %multiply_convert_fusion.3 = (bf16[256,512]{1,0:T(8,128)(2,1)S(1)}, f32[256,512]{1,0:T(8,128)}) fusion(f32[256,512]{1,0:T(8,128)S(1)} %fusion.1, bf16[256,8192]{1,0:T(8,128)(2,1)S(1)} %copy-done.20, bf16[8192,512]{1,0:T(8,128)(2,1)} %param.8), kind=kOutput, calls=%fused_computation.528 | convolution fusion | flops 2148007936 | bytes 13893632 | tf_op jit(solution)/shard_map/dot_general | solution.py:51
  78.0 1.7 collective-permute-start
  79.8 1.7 fusion.270
  81.5 0.1 maximum_convert_fusion
  81.6 16.5 %multiply_convert_fusion.2 = (bf16[256,512]{1,0:T(8,128)(2,1)}, f32[256,512]{1,0:T(8,128)}, f32[256,512]{1,0:T(8,128)}) fusion(f32[383,512]{1,0:T(8,128)S(1)} %maximum_convert_fusion, f32[512]{0:T(512)} %bitcast.391, f32[512]{0:T(512)} %bitcast.393, f32[512]{0:T(512)S(1)} %bitcast.293, f32[512]{0:T(512)S(1)} %bitcast.295, f32[512]{0:T(512)S(1)} %bitcast.297, ...), kind=kOutput, calls=%fused_computation.526 | convolution fusion | flops 2181431296 | bytes 81264640 | tf_op jit(solution)/shard_map/dot_general | solution.py:50
  98.1 2.1 fusion.127
  100.2 0.2 fusion.126
  100.4 1.0 fusion.128
  101.4 1.0 fusion.129
  102.4 1.0 fusion.130
  103.5 1.1 fusion.131
  104.6 1.1 fusion.132
  105.6 1.0 fusion.133
  108.1 10.1 %stack.515 = bf16[1,128,512]{2,1,0:T(8,128)(2,1)} concatenate(bf16[1,1,512]{2,1,0:T(2,128)(2,1)S(1)} %stack.387, bf16[1,1,512]{2,1,0:T(2,128)(2,1)S(1)} %stack.388, bf16[1,1,512]{2,1,0:T(2,128)(2,1)S(1)} %stack.389, bf16[1,1,512]{2,1,0:T(2,128)(2,1)S(1)} %stack.390, bf16[1,1,512]{2,1,0:T(2,128)(2,1)S(1)} %stack.391, bf16[1,1,512]{2,1,0:T(2,128)(2,1)S(1)} %stack.392, ...), dimensions={1} | concatenate | bytes 262144 | tf_op jit(solution)/shard_map/stack | solution.py:35
  118.4 1.3 collective-permute-start.1
  119.8 5.8 %fusion.261 = f32[256,8192]{1,0:T(8,128)S(1)} fusion(bf16[8192,512]{1,0:T(8,128)(2,1)} %param.7, f32[256,512]{1,0:T(8,128)S(1)} %copy-done.4, bf16[256,512]{1,0:T(8,128)(2,1)S(1)} %copy-done), kind=kOutput, calls=%fused_computation.532 | convolution fusion | flops 2147876864 | bytes 17563648 | tf_op jit(solution)/shard_map/dot_general | solution.py:39
  125.6 0.1 maximum_convert_fusion.1
  125.9 12.3 %fusion.134 = f32[256,512]{1,0:T(8,128)S(1)} fusion(f32[383,512]{1,0:T(8,128)S(1)} %maximum_convert_fusion.1, f32[512]{0:T(512)S(1)} %bitcast.392, f32[512]{0:T(512)S(1)} %bitcast.394, f32[512]{0:T(512)S(1)} %bitcast.294, f32[512]{0:T(512)S(1)} %bitcast.296, f32[512]{0:T(512)S(1)} %bitcast.298, f32[512]{0:T(512)S(1)} %bitcast.300, f32[512]{0:T(512)S(1)} %bitcast.302, ...), kind=kLoop, calls=%fused_computation.270 | loop fusion | flops 33423360 | bytes 67895296 | tf_op jit(solution)/shard_map/add | solution.py:26
  138.2 9.1 %convolution_add_fusion.1 = f32[256,8192]{1,0:T(8,128)} fusion(f32[256,8192]{1,0:T(8,128)S(1)} %fusion.261, bf16[8192,512]{1,0:T(8,128)(2,1)} %param.8, f32[256,512]{1,0:T(8,128)S(1)} %fusion.134, f32[256,512]{1,0:T(8,128)S(1)} %copy-done.3), kind=kOutput, calls=%fused_computation.129 | convolution fusion | flops 2149842944 | bytes 26214400 | tf_op jit(solution)/shard_map/dot_general | solution.py:39
  147.4 10.1 %fusion = bf16[256,8192]{1,0:T(8,128)(2,1)} fusion(f32[256,8192]{1,0:T(8,128)} %convolution_add_fusion.1, bf16[8192,512]{1,0:T(8,128)(2,1)} %param.9, f32[256,512]{1,0:T(8,128)S(1)} %fusion.134, f32[256,512]{1,0:T(8,128)S(1)} %copy-done.1), kind=kOutput, calls=%fused_computation.130 | convolution fusion | flops 2151940096 | bytes 22020096 | tf_op jit(solution)/shard_map/dot_general | solution.py:39
  157.6 1.4 reduce_sum.1292
  158.9 0.7 convert_element_type.73
  159.7 78.8 %reduce-scatter.2.cloned.1.call-done = bf16[16,8192]{1,0:T(8,128)(2,1)} async-done(((bf16[256,8192]{1,0:T(8,128)(2,1)}), bf16[16,8192]{1,0:T(8,128)(2,1)}) %reduce-scatter.2.cloned.1.call-update) | async-done | bytes 262160 | tf_op jit(solution)/shard_map/reduce_scatter | solution.py:80
  (185 shorter events, 0.9 us)
Async XLA Ops:
  7.2 56.9 %all-gather.3.cloned.1.call-start = ((), (), s32[]{:S(2)}) async-start(), calls=%async_computation.1 | async-start | bytes 4456448 | tf_op jit(solution)/shard_map/all_gather | solution.py:49
  7.9 149.6 %all-gather.5.cloned.1.call-start = ((), (), s32[]{:S(2)}) async-start(), calls=%async_computation.3 | async-start | bytes 1179648 | tf_op jit(solution)/shard_map/all_gather | solution.py:72
  64.0 7.1 %copy-start.20 = (bf16[256,8192]{1,0:T(8,128)(2,1)S(1)}, bf16[256,8192]{1,0:T(8,128)(2,1)}, u32[]{:S(2)}) copy-start(bf16[256,8192]{1,0:T(8,128)(2,1)} %all-gather.3.cloned.1.call-done) | copy-start | bytes 12582916
  64.0 17.5 %slice-start = ((s8[8388608]{0:T(1024)(128)(4,1)}), s8[4194304]{0:T(1024)(128)(4,1)S(1)}, s32[]{:S(2)}) async-start(s8[8388608]{0:T(1024)(128)(4,1)} %bitcast.137), calls=%async_computation.4 | async-start | bytes 8388608
  71.2 6.8 %copy-start.2 = (f32[256,512]{1,0:T(8,128)}, f32[256,512]{1,0:T(8,128)S(1)}, u32[]{:S(2)}) copy-start(f32[256,512]{1,0:T(8,128)S(1)} %fusion.1) | copy-start | bytes 1572868
  71.2 10.4 %slice-start.1 = ((s8[8388608]{0:T(1024)(128)(4,1)}), s8[4194304]{0:T(1024)(128)(4,1)S(1)}, s32[]{:S(2)}) async-start(s8[8388608]{0:T(1024)(128)(4,1)} %bitcast.137), calls=%async_computation.5 | async-start | bytes 8388608
  78.0 3.4 %collective-permute-start = (bf16[127,512]{1,0:T(8,128)(2,1)S(1)}, bf16[127,512]{1,0:T(8,128)(2,1)S(1)}, u32[]{:S(2)}, u32[]{:S(2)}) collective-permute-start(bf16[127,512]{1,0:T(8,128)(2,1)S(1)} %slice.1812), channel_id=1, source_target_pairs={{0,16},{16,32},{32,48},{48,64},{64,80},{80,96},{96,112},{1,17},{17... | collective-permute-start | bytes 390152 | tf_op jit(solution)/shard_map/ppermute | solution.py:10
  81.6 16.6 %copy-start = (bf16[256,512]{1,0:T(8,128)(2,1)S(1)}, bf16[256,512]{1,0:T(8,128)(2,1)}, u32[]{:S(2)}) copy-start(bf16[256,512]{1,0:T(8,128)(2,1)} %param.11) | copy-start | bytes 786436
  104.5 15.1 %copy-start.4 = (f32[256,512]{1,0:T(8,128)S(1)}, f32[256,512]{1,0:T(8,128)}, u32[]{:S(2)}) copy-start(f32[256,512]{1,0:T(8,128)} %get-tuple-element.133) | copy-start | bytes 1572868
  118.3 120.1 %reduce-scatter.2.cloned.1.call-start = ((), (), s32[]{:S(2)}) async-start(), calls=%async_computation.2 | async-start | bytes 4456448 | tf_op jit(solution)/shard_map/reduce_scatter | solution.py:80
  118.4 7.2 %collective-permute-start.1 = (bf16[127,512]{1,0:T(8,128)(2,1)S(1)}, bf16[127,512]{1,0:T(8,128)(2,1)S(1)}, u32[]{:S(2)}, u32[]{:S(2)}) collective-permute-start(bf16[127,512]{1,0:T(8,128)(2,1)S(1)} %slice.1941), channel_id=1, source_target_pairs={{16,0},{32,16},{48,32},{64,48},{80,64},{96,80},{112,96},{17,1},{33... | collective-permute-start | bytes 390152 | tf_op jit(solution)/shard_map/ppermute | solution.py:10
  119.7 6.0 %copy-start.5 = (f32[1,512]{1,0:T(1,128)S(1)}, f32[1,512]{1,0:T(1,128)}, u32[]{:S(2)}) copy-start(f32[1,512]{1,0:T(1,128)} %get-tuple-element.247) | copy-start | bytes 6148
  119.7 6.0 %copy-start.6 = (f32[1,512]{1,0:T(1,128)S(1)}, f32[1,512]{1,0:T(1,128)}, u32[]{:S(2)}) copy-start(f32[1,512]{1,0:T(1,128)} %get-tuple-element.248) | copy-start | bytes 6148
  119.7 6.0 %copy-start.7 = (f32[1,512]{1,0:T(1,128)S(1)}, f32[1,512]{1,0:T(1,128)}, u32[]{:S(2)}) copy-start(f32[1,512]{1,0:T(1,128)} %get-tuple-element.249) | copy-start | bytes 6148
  119.7 6.0 %copy-start.8 = (f32[1,512]{1,0:T(1,128)S(1)}, f32[1,512]{1,0:T(1,128)}, u32[]{:S(2)}) copy-start(f32[1,512]{1,0:T(1,128)} %get-tuple-element.250) | copy-start | bytes 6148
  119.7 6.0 %copy-start.9 = (f32[1,512]{1,0:T(1,128)S(1)}, f32[1,512]{1,0:T(1,128)}, u32[]{:S(2)}) copy-start(f32[1,512]{1,0:T(1,128)} %get-tuple-element.251) | copy-start | bytes 6148
  119.7 6.0 %copy-start.10 = (f32[1,512]{1,0:T(1,128)S(1)}, f32[1,512]{1,0:T(1,128)}, u32[]{:S(2)}) copy-start(f32[1,512]{1,0:T(1,128)} %get-tuple-element.252) | copy-start | bytes 6148
  119.7 6.0 %copy-start.11 = (f32[1,512]{1,0:T(1,128)S(1)}, f32[1,512]{1,0:T(1,128)}, u32[]{:S(2)}) copy-start(f32[1,512]{1,0:T(1,128)} %get-tuple-element.253) | copy-start | bytes 6148
  119.7 6.0 %copy-start.12 = (f32[1,512]{1,0:T(1,128)S(1)}, f32[1,512]{1,0:T(1,128)}, u32[]{:S(2)}) copy-start(f32[1,512]{1,0:T(1,128)} %get-tuple-element.254) | copy-start | bytes 6148
  119.7 6.0 %copy-start.13 = (f32[1,512]{1,0:T(1,128)S(1)}, f32[1,512]{1,0:T(1,128)}, u32[]{:S(2)}) copy-start(f32[1,512]{1,0:T(1,128)} %get-tuple-element.255) | copy-start | bytes 6148
  119.8 6.0 %copy-start.14 = (f32[1,512]{1,0:T(1,128)S(1)}, f32[1,512]{1,0:T(1,128)}, u32[]{:S(2)}) copy-start(f32[1,512]{1,0:T(1,128)} %get-tuple-element.256) | copy-start | bytes 6148
  119.8 6.0 %copy-start.15 = (f32[1,512]{1,0:T(1,128)S(1)}, f32[1,512]{1,0:T(1,128)}, u32[]{:S(2)}) copy-start(f32[1,512]{1,0:T(1,128)} %get-tuple-element.257) | copy-start | bytes 6148
  119.8 6.0 %copy-start.16 = (f32[1,512]{1,0:T(1,128)S(1)}, f32[1,512]{1,0:T(1,128)}, u32[]{:S(2)}) copy-start(f32[1,512]{1,0:T(1,128)} %get-tuple-element.258) | copy-start | bytes 6148
  119.8 6.0 %copy-start.17 = (f32[1,512]{1,0:T(1,128)S(1)}, f32[1,512]{1,0:T(1,128)}, u32[]{:S(2)}) copy-start(f32[1,512]{1,0:T(1,128)} %get-tuple-element.259) | copy-start | bytes 6148
  119.8 6.0 %copy-start.18 = (f32[1,512]{1,0:T(1,128)S(1)}, f32[1,512]{1,0:T(1,128)}, u32[]{:S(2)}) copy-start(f32[1,512]{1,0:T(1,128)} %get-tuple-element.260) | copy-start | bytes 6148
  119.8 6.0 %copy-start.19 = (f32[1,512]{1,0:T(1,128)S(1)}, f32[1,512]{1,0:T(1,128)}, u32[]{:S(2)}) copy-start(f32[1,512]{1,0:T(1,128)} %get-tuple-element.261) | copy-start | bytes 6148
  125.8 12.4 %copy-start.3 = (f32[256,512]{1,0:T(8,128)S(1)}, f32[256,512]{1,0:T(8,128)}, u32[]{:S(2)}) copy-start(f32[256,512]{1,0:T(8,128)} %copy-done.2) | copy-start | bytes 1572868
  138.2 9.2 %copy-start.1 = (f32[256,512]{1,0:T(8,128)S(1)}, f32[256,512]{1,0:T(8,128)}, u32[]{:S(2)}) copy-start(f32[256,512]{1,0:T(8,128)} %get-tuple-element.263) | copy-start | bytes 1572868
Sparse Core Ops, SparseCore 0:
  10.1 53.8 all-gather.2
  118.4 26.1 all-gather.4
  157.6 80.7 reduce-scatter.1
